TPU v7x, 32 devices: a whole 2x2x4 slice. The times are simulated.
32 devices in a mesh: row: 8 (over z, x), col: 4 (over y, core).
Axes of the slice: x: 2, y: 2, z: 4, core: 2. Of those that a mesh axis runs over, the one named last changes fastest.
Arguments:
- panel: float32 [8, 16384, 4, 1024], P('row', None, 'col'), may hold values from -1 to 4, as said below
- rhs: float32 [8, 16384, 256], P('row'), may hold values from -6 to 6
Outputs:
- solved: float32 [4, 1024, 256], P('col')
- remainder: float32 [8, 16384, 256], P('row', None, 'col')
Inputs may be any that keep to these rules, and one draw needn't show every extreme that they name: panel is lower triangular in the global indices: entries with column above row are zero, diagonal entries lie between 2 and 4, the others are of size about 1 / sqrt(4096).
All inputs are finite; a program needn't handle non-finite values.
Results may differ from a plain program's by a relative error of at most 0.000084.
Values sent between devices are 32-bit elements; how exact they have to be, the bound alone decides.
A program may use at most 256 MiB of HBM per device.

v0:
```python
import jax
import jax.numpy as jnp
from jax import lax
from jax.sharding import PartitionSpec as P

TB = 512
STEPS = 8


def broadcast(value, axis, root):
    mine = lax.axis_index(axis) == root
    return lax.psum(jnp.where(mine, value, jnp.zeros_like(value)), axis)


def multiply(left, right):
    return jnp.dot(left, right, precision=lax.Precision.HIGHEST, preferred_element_type=jnp.float32)


def solve_block(matrix, values):
    return lax.linalg.triangular_solve(matrix, values, left_side=True, lower=True)


def on_device(panel, rhs):
    row_count = lax.axis_size("row")
    col_count = lax.axis_size("col")
    here_row = lax.axis_index("row")
    here_col = lax.axis_index("col")
    local_panel = panel.reshape(panel.shape[1], panel.shape[3])
    right_side = rhs.reshape(rhs.shape[1], rhs.shape[2])
    tile_cols = local_panel.shape[1] // TB
    identity = jnp.eye(TB, dtype=jnp.float32)
    solved = []
    for step in range(STEPS):
        owner_row = step % row_count
        owner_col = step % col_count
        tile_row = step // row_count
        tile_col = step // col_count
        row_lo = tile_row * TB
        partial_value = jnp.zeros((TB, right_side.shape[1]), jnp.float32)
        if step > 0:
            solved_stack = jnp.stack(solved)
            for column_tile in range(tile_cols):
                tile_index = column_tile * col_count + here_col
                picked = lax.dynamic_index_in_dim(
                    solved_stack, jnp.clip(tile_index, 0, step - 1), 0, keepdims=False
                )
                update = multiply(
                    local_panel[row_lo : row_lo + TB, column_tile * TB : (column_tile + 1) * TB],
                    picked,
                )
                partial_value = partial_value + jnp.where(tile_index < step, update, 0.0)
        block_rhs = right_side[row_lo : row_lo + TB]
        summed_part = lax.psum(partial_value, "col")
        is_owner = jnp.logical_and(here_row == owner_row, here_col == owner_col)
        diag_local = jnp.where(
            is_owner,
            local_panel[row_lo : row_lo + TB, tile_col * TB : (tile_col + 1) * TB],
            identity,
        )
        solution_block = broadcast(
            solve_block(diag_local, block_rhs - summed_part), "row", owner_row
        )
        solved.append(solution_block)
    solved_stack = jnp.stack(solved)
    own_blocks = [
        lax.dynamic_index_in_dim(
            solved_stack, column_tile * col_count + here_col, 0, keepdims=False
        )
        for column_tile in range(tile_cols)
    ]
    own_solved = jnp.concatenate(own_blocks, 0)
    running_sum = multiply(local_panel, own_solved)
    rhs_split = right_side.shape[1] // col_count
    reduced = lax.psum_scatter(running_sum, "col", scatter_dimension=1, tiled=True)
    own_columns = lax.dynamic_slice_in_dim(right_side, here_col * rhs_split, rhs_split, 1)
    remainder = (own_columns - reduced).reshape(1, right_side.shape[0], rhs_split)
    return (own_solved.reshape(1, own_solved.shape[0], own_solved.shape[1]), remainder)


def solution(mesh):
    return jax.shard_map(
        on_device,
        mesh=mesh,
        in_specs=(P("row", None, "col", None), P("row", None, None)),
        out_specs=(P("col", None, None), P("row", None, "col")),
        check_vma=False,
    )
```

profile of v0, /device:TPU:0, one launch (start us, length us, event | category | flops | bytes accessed | tf_op | source)
XLA Modules:
  0.0 1419.5 jit_solution(8562701969189474530)
XLA Ops:
  7.3 44.1 %copy.11 = f32[1,16384,1,1024]{3,1,2,0:T(8,128)} copy(f32[1,16384,1,1024]{3,2,1,0:T(1,128)} %param.4) | data formatting | bytes 134217728
  51.4 4.8 fusion.22
  56.2 7.8 while.16
  64.0 39.3 %custom-call.10 = f32[4,128,128]{1,2,0:T(8,128)S(1)} custom-call(f32[4,128,128]{2,1,0:T(8,128)S(1)} %get-tuple-element.53), custom_call_target="InvertDiagBlocksLowerTriangular" | custom-call | tf_op jit(solution)/shard_map/triangular_solve/custom-call.1 | solution.py:20
  107.5 75.6 %all-reduce.16.cloned.1.call-done = f32[512,256]{1,0:T(8,128)} async-done(((f32[512,256]{1,0:T(8,128)}), f32[512,256]{1,0:T(8,128)}) %all-reduce.16.cloned.1.call-update) | async-done | bytes 524304 | tf_op jit(solution)/shard_map/psum | solution.py:12
  183.1 3.3 convolution_select_fusion.13
  186.3 4.1 fusion.14
  190.7 12.2 while.17
  194.5 2.4 bitcast_dynamic-update-slice_fusion.17
  197.6 2.4 bitcast_dynamic-update-slice_fusion.17
  203.0 39.3 %custom-call.11 = f32[4,128,128]{1,2,0:T(8,128)S(1)} custom-call(f32[4,128,128]{2,1,0:T(8,128)S(1)} %get-tuple-element.54), custom_call_target="InvertDiagBlocksLowerTriangular" | custom-call | tf_op jit(solution)/shard_map/triangular_solve/custom-call.1 | solution.py:20
  250.1 72.0 %all-reduce.20.cloned.1.call-done = f32[1,512,256]{2,1,0:T(8,128)} async-done(((f32[1,512,256]{2,1,0:T(8,128)}), f32[1,512,256]{2,1,0:T(8,128)}) %all-reduce.20.cloned.1.call-update) | async-done | bytes 524304 | tf_op jit(solution)/shard_map/psum | solution.py:12
  322.1 3.1 convolution_select_fusion.11
  325.3 4.1 fusion.12
  329.9 12.2 while.18
  342.1 39.3 %custom-call.12 = f32[4,128,128]{1,2,0:T(8,128)S(1)} custom-call(f32[4,128,128]{2,1,0:T(8,128)S(1)} %get-tuple-element.55), custom_call_target="InvertDiagBlocksLowerTriangular" | custom-call | tf_op jit(solution)/shard_map/triangular_solve/custom-call.1 | solution.py:20
  389.2 72.2 %all-reduce.24.cloned.1.call-done = f32[1,512,256]{2,1,0:T(8,128)} async-done(((f32[1,512,256]{2,1,0:T(8,128)}), f32[1,512,256]{2,1,0:T(8,128)}) %all-reduce.24.cloned.1.call-update) | async-done | bytes 524304 | tf_op jit(solution)/shard_map/psum | solution.py:12
  462.6 3.1 convolution_select_fusion.9
  465.7 3.9 fusion.10
  469.9 11.4 while.19
  482.0 40.1 %custom-call.13 = f32[4,128,128]{1,2,0:T(8,128)S(1)} custom-call(f32[4,128,128]{2,1,0:T(8,128)} %copy-done.4), custom_call_target="InvertDiagBlocksLowerTriangular" | custom-call | tf_op jit(solution)/shard_map/triangular_solve/custom-call.1 | solution.py:20
  529.9 71.9 %all-reduce.28.cloned.1.call-done = f32[1,512,256]{2,1,0:T(8,128)} async-done(((f32[1,512,256]{2,1,0:T(8,128)}), f32[1,512,256]{2,1,0:T(8,128)}) %all-reduce.28.cloned.1.call-update) | async-done | bytes 524304 | tf_op jit(solution)/shard_map/psum | solution.py:12
  603.0 3.2 convolution_select_fusion.7
  606.1 4.0 fusion.8
  610.4 11.7 while.20
  622.8 40.1 %custom-call.14 = f32[4,128,128]{1,2,0:T(8,128)S(1)} custom-call(f32[4,128,128]{2,1,0:T(8,128)} %copy-done.5), custom_call_target="InvertDiagBlocksLowerTriangular" | custom-call | tf_op jit(solution)/shard_map/triangular_solve/custom-call.1 | solution.py:20
  676.8 66.0 %all-reduce.32.cloned.1.call-done = f32[1,512,256]{2,1,0:T(8,128)} async-done(((f32[1,512,256]{2,1,0:T(8,128)}), f32[1,512,256]{2,1,0:T(8,128)}) %all-reduce.32.cloned.1.call-update) | async-done | bytes 524304 | tf_op jit(solution)/shard_map/psum | solution.py:12
  742.8 2.5 constant_dynamic-update-slice_fusion.13
  745.3 3.3 convolution_select_fusion.5
  748.6 4.1 fusion.6
  753.1 12.0 while.21
  765.1 39.3 %custom-call.15 = f32[4,128,128]{1,2,0:T(8,128)S(1)} custom-call(f32[4,128,128]{2,1,0:T(8,128)S(1)} %get-tuple-element.58), custom_call_target="InvertDiagBlocksLowerTriangular" | custom-call | tf_op jit(solution)/shard_map/triangular_solve/custom-call.1 | solution.py:20
  812.2 71.9 %all-reduce.36.cloned.1.call-done = f32[1,512,256]{2,1,0:T(8,128)} async-done(((f32[1,512,256]{2,1,0:T(8,128)}), f32[1,512,256]{2,1,0:T(8,128)}) %all-reduce.36.cloned.1.call-update) | async-done | bytes 524304 | tf_op jit(solution)/shard_map/psum | solution.py:12
  886.5 3.3 convolution_select_fusion.3
  889.8 4.1 fusion.4
  894.1 11.6 while.22
  905.7 39.3 %custom-call.16 = f32[4,128,128]{1,2,0:T(8,128)S(1)} custom-call(f32[4,128,128]{2,1,0:T(8,128)S(1)} %get-tuple-element.59), custom_call_target="InvertDiagBlocksLowerTriangular" | custom-call | tf_op jit(solution)/shard_map/triangular_solve/custom-call.1 | solution.py:20
  952.9 72.0 %all-reduce.40.cloned.1.call-done = f32[1,512,256]{2,1,0:T(8,128)} async-done(((f32[1,512,256]{2,1,0:T(8,128)}), f32[1,512,256]{2,1,0:T(8,128)}) %all-reduce.40.cloned.1.call-update) | async-done | bytes 524304 | tf_op jit(solution)/shard_map/psum | solution.py:12
  1026.9 3.3 convolution_select_fusion.1
  1030.2 4.1 fusion.2
  1034.3 8.1 while.23
  1042.5 39.3 %custom-call.17 = f32[4,128,128]{1,2,0:T(8,128)S(1)} custom-call(f32[4,128,128]{2,1,0:T(8,128)S(1)} %get-tuple-element.60), custom_call_target="InvertDiagBlocksLowerTriangular" | custom-call | tf_op jit(solution)/shard_map/triangular_solve/custom-call.1 | solution.py:20
  1086.9 72.1 %all-reduce.44.cloned.1.call-done = f32[1,512,256]{2,1,0:T(8,128)} async-done(((f32[1,512,256]{2,1,0:T(8,128)}), f32[1,512,256]{2,1,0:T(8,128)}) %all-reduce.44.cloned.1.call-update) | async-done | bytes 524304 | tf_op jit(solution)/shard_map/psum | solution.py:12
  1162.2 120.1 %convolution_bitcast_fusion = f32[16384,256]{0,1:T(8,128)} fusion(f32[512,256]{1,0:T(8,128)S(1)} %get-tuple-element.150, f32[512,256]{1,0:T(8,128)S(1)} %get-tuple-element.149, f32[1,16384,1,1024]{3,2,1,0:T(1,128)} %param.4), kind=kOutput, calls=%fused_computation.17 | convolution fusion | flops 51539869696 | bytes 84934656 | tf_op jit(solution)/shard_map/dot_general | solution.py:16
  1282.3 7.1 constant_dynamic-slice_fusion.8
  1289.4 8.4 copy.5
  1298.8 107.8 %reduce-scatter.2.cloned.1.call-done = f32[16384,64]{0,1:T(8,128)} async-done(((f32[16384,256]{0,1:T(8,128)}), f32[16384,64]{0,1:T(8,128)}) %reduce-scatter.2.cloned.1.call-update) | async-done | bytes 4194320 | tf_op jit(solution)/shard_map/reduce_scatter | solution.py:74
  1406.7 5.9 fusion
  (240 shorter events, 157.8 us)
Async XLA Ops:
  7.2 175.9 %all-reduce.16.cloned.1.call-start = ((), (), s32[]{:S(2)}) async-start(), calls=%async_computation.1 | async-start | bytes 1048576 | tf_op jit(solution)/shard_map/psum | solution.py:12
  51.4 51.9 %slice-start = ((f32[1,16384,256]{2,1,0:T(8,128)}), f32[1,512,256]{2,1,0:T(8,128)S(1)}, s32[]{:S(2)}) async-start(f32[1,16384,256]{2,1,0:T(8,128)} %param.5), calls=%async_computation.17 | async-start | bytes 1048576 | tf_op jit(solution)/shard_map/slice | solution.py:52
  107.4 134.9 %all-reduce.18.cloned.1.call-start = ((), (), s32[]{:S(2)}) async-start(), calls=%async_computation.2 | async-start | bytes 1048576 | tf_op jit(solution)/shard_map/psum | solution.py:53
  190.4 131.7 %all-reduce.20.cloned.1.call-start = ((), (), s32[]{:S(2)}) async-start(), calls=%async_computation.3 | async-start | bytes 1048576 | tf_op jit(solution)/shard_map/psum | solution.py:12
  190.7 131.4 %copy-start = (f32[512,256]{1,0:T(8,128)S(1)}, f32[512,256]{1,0:T(8,128)}, u32[]{:S(2)}) copy-start(f32[512,256]{1,0:T(8,128)} %all-reduce.16.cloned.1.call-done) | copy-start | bytes 1572868
  250.1 131.4 %all-reduce.22.cloned.1.call-start = ((), (), s32[]{:S(2)}) async-start(), calls=%async_computation.4 | async-start | bytes 1048576 | tf_op jit(solution)/shard_map/psum | solution.py:53
  329.4 132.1 %all-reduce.24.cloned.1.call-start = ((), (), s32[]{:S(2)}) async-start(), calls=%async_computation.5 | async-start | bytes 1048576 | tf_op jit(solution)/shard_map/psum | solution.py:12
  329.9 131.6 %copy-start.1 = (f32[1,512,256]{2,1,0:T(8,128)S(1)}, f32[1,512,256]{2,1,0:T(8,128)}, u32[]{:S(2)}) copy-start(f32[1,512,256]{2,1,0:T(8,128)} %all-reduce.20.cloned.1.call-done) | copy-start | bytes 1572868
  389.2 132.9 %all-reduce.26.cloned.1.call-start = ((), (), s32[]{:S(2)}) async-start(), calls=%async_computation.6 | async-start | bytes 1048576 | tf_op jit(solution)/shard_map/psum | solution.py:53
  469.6 132.2 %all-reduce.28.cloned.1.call-start = ((), (), s32[]{:S(2)}) async-start(), calls=%async_computation.7 | async-start | bytes 1048576 | tf_op jit(solution)/shard_map/psum | solution.py:12
  469.9 131.9 %copy-start.2 = (f32[1,512,256]{2,1,0:T(8,128)S(1)}, f32[1,512,256]{2,1,0:T(8,128)}, u32[]{:S(2)}) copy-start(f32[1,512,256]{2,1,0:T(8,128)} %all-reduce.24.cloned.1.call-done) | copy-start | bytes 1572868
  481.2 0.7 copy-start.4
  529.9 133.1 %all-reduce.30.cloned.1.call-start = ((), (), s32[]{:S(2)}) async-start(), calls=%async_computation.8 | async-start | bytes 1048576 | tf_op jit(solution)/shard_map/psum | solution.py:53
  610.1 132.7 %all-reduce.32.cloned.1.call-start = ((), (), s32[]{:S(2)}) async-start(), calls=%async_computation.9 | async-start | bytes 1048576 | tf_op jit(solution)/shard_map/psum | solution.py:12
  622.1 0.7 copy-start.5
  670.7 133.8 %all-reduce.34.cloned.1.call-start = ((), (), s32[]{:S(2)}) async-start(), calls=%async_computation.10 | async-start | bytes 1048576 | tf_op jit(solution)/shard_map/psum | solution.py:53
  670.7 4.5 copy-start.3
  752.6 131.5 %all-reduce.36.cloned.1.call-start = ((), (), s32[]{:S(2)}) async-start(), calls=%async_computation.11 | async-start | bytes 1048576 | tf_op jit(solution)/shard_map/psum | solution.py:12
  812.2 132.9 %all-reduce.38.cloned.1.call-start = ((), (), s32[]{:S(2)}) async-start(), calls=%async_computation.12 | async-start | bytes 1048576 | tf_op jit(solution)/shard_map/psum | solution.py:53
  893.8 131.0 %all-reduce.40.cloned.1.call-start = ((), (), s32[]{:S(2)}) async-start(), calls=%async_computation.13 | async-start | bytes 1048576 | tf_op jit(solution)/shard_map/psum | solution.py:12
  952.8 129.0 %all-reduce.42.cloned.1.call-start = ((), (), s32[]{:S(2)}) async-start(), calls=%async_computation.14 | async-start | bytes 1048576 | tf_op jit(solution)/shard_map/psum | solution.py:53
  1034.3 124.8 %all-reduce.44.cloned.1.call-start = ((), (), s32[]{:S(2)}) async-start(), calls=%async_computation.15 | async-start | bytes 1048576 | tf_op jit(solution)/shard_map/psum | solution.py:12
  1086.9 319.8 %reduce-scatter.2.cloned.1.call-start = ((), (), s32[]{:S(2)}) async-start(), calls=%async_computation.16 | async-start | bytes 20971520 | tf_op jit(solution)/shard_map/reduce_scatter | solution.py:74
Sparse Core Ops, SparseCore 0:
  107.6 75.4 all-reduce.15
  190.5 33.4 all-reduce.17
  250.2 71.9 all-reduce.19
  329.5 32.9 all-reduce.21
  389.3 72.1 all-reduce.23
  469.7 33.3 all-reduce.25
  530.0 71.7 all-reduce.27
  610.2 32.9 all-reduce.29
  670.8 71.9 all-reduce.31
  752.8 33.3 all-reduce.33
  812.3 71.8 all-reduce.35
  894.0 32.8 all-reduce.37
  952.9 71.8 all-reduce.39
  1034.4 33.3 all-reduce.41
  1087.0 71.9 all-reduce.43
  1282.4 124.2 reduce-scatter.1
where the time goes:
time: 1430 us; the launch traced here: 1420 us
  waiting for transfers between devices  682 us (48%)
  other arithmetic  345 us (24%)
  matrix products  211 us (15%)
  local copies, waits for them, and re-layouts  164 us (11%)
  between operations  15.2 us (1%)
    psum x8, waiting for transfers between devices, broadcast(): return lax.psum(jnp.where(mine, value, jnp.zeros_like(value)), axis)  574 us
    another operation x10, other arithmetic, solve_block(): lax.linalg.triangular_solve(matrix, values, left_side=True, lower=True)  321 us
    dot_general x15, matrix products, multiply(): jnp.dot(left, right, precision=lax.Precision.HIGHEST, preferred_element_t...  171 us
    reduce_scatter x1, waiting for transfers between devices, on_device(): lax.psum_scatter(running_sum, 'col', scatter_dimension=1, tiled=True)  108 us
    another operation x105, local copies, waits for them, and re-layouts, solve_block(): lax.linalg.triangular_solve(matrix, values, left_side=True, lower=True)  86.5 us
    unnamed x20, local copies, waits for them, and re-layouts  56.6 us
    another operation x56, matrix products, solve_block(): lax.linalg.triangular_solve(matrix, values, left_side=True, lower=True)  40.4 us
  transfers between devices with their start and end apart: 16, of which 9 were waited for; matrix products, arithmetic and copies ran while one was open for 27% of the time, Pallas kernels for 0%

commit v1 on v0

v1 whole, which is shorter than its diff:
```python
import jax
import jax.numpy as jnp
from jax import lax
from jax.sharding import PartitionSpec as P

TB = 512
BASE = 128
CHUNKS = 4
LANES = 128


def dot(left, right, precision=lax.Precision.HIGHEST):
    return jnp.matmul(left, right, precision=precision, preferred_element_type=jnp.float32)


def invert_lower(tile):
    size = tile.shape[0]
    count = size // BASE
    blocks = jnp.stack(
        [tile[i * BASE : (i + 1) * BASE, i * BASE : (i + 1) * BASE] for i in range(count)]
    )
    eye = jnp.eye(BASE, dtype=jnp.float32)
    scale = 1.0 / jnp.sum(blocks * eye, axis=2)
    power = -jnp.tril(blocks * scale[:, :, None], -1)
    inverse = eye + power
    reach = 2
    while reach < BASE:
        power = dot(power, power)
        inverse = inverse + dot(inverse, power)
        reach *= 2
    inverse = inverse * scale[:, None, :]
    parts = [inverse[i] for i in range(count)]
    width = BASE
    while len(parts) > 1:
        merged = []
        for i in range(0, len(parts), 2):
            lo = i * width
            below = tile[lo + width : lo + 2 * width, lo : lo + width]
            corner = -dot(parts[i + 1], dot(below, parts[i]))
            top = jnp.concatenate([parts[i], jnp.zeros_like(corner)], 1)
            merged.append(jnp.concatenate([top, jnp.concatenate([corner, parts[i + 1]], 1)], 0))
        parts = merged
        width *= 2
    return parts[0]


def pack(value, factor):
    rows = value.shape[0] // factor
    return jnp.concatenate([value[i * rows : (i + 1) * rows] for i in range(factor)], 1)


def unpack(value, factor):
    width = value.shape[1] // factor
    return jnp.concatenate([value[:, i * width : (i + 1) * width] for i in range(factor)], 0)


def on_device(panel, rhs):
    col_count = lax.axis_size("col")
    here_row = lax.axis_index("row")
    here_col = lax.axis_index("col")
    local_panel = panel.reshape(panel.shape[1], panel.shape[3])
    right_side = rhs.reshape(rhs.shape[1], rhs.shape[2])
    rows, width = right_side.shape
    tile_cols = local_panel.shape[1] // TB
    steps = tile_cols * col_count

    top = local_panel[:TB]
    diag_col = jnp.minimum(here_row // col_count, tile_cols - 1)
    has_diag = jnp.logical_and(here_row < steps, here_row % col_count == here_col)
    picked = lax.dynamic_slice_in_dim(top, diag_col * TB, TB, 1)
    diag = lax.psum(jnp.where(has_diag, picked, 0.0), "col")
    diag = jnp.where(here_row < steps, diag, jnp.eye(TB, dtype=jnp.float32))
    inverse = invert_lower(diag)
    tile_of = (jnp.arange(tile_cols * TB) // TB) * col_count + here_col
    coupling = dot(inverse, jnp.where((tile_of < here_row)[None, :], top, 0.0))
    direct = jnp.where(has_diag, dot(inverse, right_side[:TB]), 0.0)

    own = [jnp.zeros((TB, width), jnp.float32) for _ in range(tile_cols)]
    for step in range(steps):
        term = direct
        known = -(-step // col_count)
        if known:
            stacked = own[0] if known == 1 else jnp.concatenate(own[:known], 0)
            term = direct - dot(coupling[:, : known * TB], stacked)
        block = lax.psum(jnp.where(here_row == step, term, 0.0), ("row", "col"))
        place = step // col_count
        own[place] = jnp.where(here_col == step % col_count, block, own[place])
    own_solved = own[0] if tile_cols == 1 else jnp.concatenate(own, 0)

    chips = col_count // 2
    part = width // col_count
    half = width // 2
    factor = max(1, LANES // part)
    chip = here_col // 2
    core = here_col % 2

    def columns(target_core, hop):
        target = lax.rem(chip - 1 - hop + 2 * chips, chips) * 2 + target_core
        return lax.dynamic_slice_in_dim(own_solved, target * part, part, 1)

    order = [columns(1 - core, hop) for hop in range(chips)]
    order += [columns(core, hop) for hop in range(chips)]
    weights = jnp.concatenate(order, 1)
    swap = [(c, c ^ 1) for c in range(col_count)]
    ring = [(c, (c + 2) % col_count) for c in range(col_count)]
    size = rows // CHUNKS
    pieces = []
    for chunk in range(CHUNKS):
        lo = chunk * size
        product = dot(local_panel[lo : lo + size], weights, lax.Precision.HIGH)
        paired = product[:, half:] + lax.ppermute(product[:, :half], "col", swap)
        total = pack(paired[:, :part], factor)
        for hop in range(1, chips):
            total = lax.ppermute(total, "col", ring)
            total = total + pack(paired[:, hop * part : (hop + 1) * part], factor)
        mine = lax.dynamic_slice(right_side, (lo, here_col * part), (size, part))
        pieces.append(mine - unpack(total, factor))
    remainder = jnp.concatenate(pieces, 0)
    return own_solved[None], remainder[None]


def solution(mesh):
    return jax.shard_map(
        on_device,
        mesh=mesh,
        in_specs=(P("row", None, "col", None), P("row", None, None)),
        out_specs=(P("col", None, None), P("row", None, "col")),
        check_vma=False,
    )
```

time: 1430 us -> 1330 us (0.930)
  waiting for transfers between devices: 682 us -> 1090 us
  other arithmetic: 345 us -> 18.2 us
  matrix products: 211 us -> 97.8 us
  local copies, waits for them, and re-layouts: 164 us -> 83.9 us
  starting transfers between devices: 2.24 us -> 18 us
    psum x15 -> x9, waiting for transfers between devices: 574 us -> 1000 us  [the longest x8 963 us: on_device(): block = lax.psum(jnp.where(here_row == step, term, 0.0), ('row', 'col'))]
    another operation x19 -> x0, other arithmetic: 329 us -> none  [the longest x10 321 us: solve_block(): lax.linalg.triangular_solve(matrix, values, left_side=True, lower=True)]
    reduce_scatter x1 -> x0, waiting for transfers between devices: 108 us -> none  [on_device(): lax.psum_scatter(running_sum, 'col', scatter_dimension=1, tiled=True)]
    another operation x107 -> x1, local copies, waits for them, and re-layouts: 90.4 us -> 0.02 us  [invert_lower(): jnp.stack([tile[i * BASE:(i + 1) * BASE, i * BASE:(i + 1) * BASE] for i i...]
    ppermute x0 -> x8, waiting for transfers between devices: none -> 82.9 us  [the longest x4 82.9 us: on_device(): total = lax.ppermute(total, 'col', ring)]
    dot_general x15 -> x31, matrix products: 171 us -> 97.8 us  [dot(): jnp.matmul(left, right, precision=precision, preferred_element_type=jnp.f...]
    slice x2 -> x14, local copies, waits for them, and re-layouts: 0.01 us -> 53.2 us  [the longest x1 44.1 us: on_device(): product = dot(local_panel[lo:lo + size], weights, lax.Precision.HIGH)]
    unnamed x20 -> x47, local copies, waits for them, and re-layouts: 56.6 us -> 11.2 us
  transfers between devices with their start and end apart: 16 -> 17, of which waited for: 9 -> 13; matrix products, arithmetic and copies ran while one was open for 27% -> 10% of each run, Pallas kernels for 0% -> 0%
where the time goes in v1:
time: 1330 us; the launch traced here: 1320 us
  waiting for transfers between devices  1090 us (82%)
  matrix products  97.8 us (7%)
  local copies, waits for them, and re-layouts  83.9 us (6%)
  other arithmetic  18.2 us (1%)
  starting transfers between devices  18 us (1%)
  between operations  15.1 us (1%)
    psum x8, waiting for transfers between devices, on_device(): block = lax.psum(jnp.where(here_row == step, term, 0.0), ('row', 'col'))  963 us
    dot_general x31, matrix products, dot(): jnp.matmul(left, right, precision=precision, preferred_element_type=jnp.f...  97.8 us
    ppermute x4, waiting for transfers between devices, on_device(): total = lax.ppermute(total, 'col', ring)  82.9 us
    slice x1, local copies, waits for them, and re-layouts, on_device(): product = dot(local_panel[lo:lo + size], weights, lax.Precision.HIGH)  44.1 us
    psum x1, waiting for transfers between devices, on_device(): diag = lax.psum(jnp.where(has_diag, picked, 0.0), 'col')  39 us
  transfers between devices with their start and end apart: 17, of which 13 were waited for; matrix products, arithmetic and copies ran while one was open for 10% of the time, Pallas kernels for 0%

profile of v1, /device:TPU:0, one launch (start us, length us, event | category | flops | bytes accessed | tf_op | source)
XLA Modules:
  0.0 1318.2 jit_solution(84741691303237066)
XLA Ops:
  7.2 3.0 slice.195
  10.3 1.3 copy-done.6
  13.4 39.0 %all-reduce.13.cloned.1.call-done = f32[512,512]{1,0:T(8,128)} async-done(((f32[512,512]{1,0:T(8,128)}), f32[512,512]{1,0:T(8,128)}) %all-reduce.13.cloned.1.call-update) | async-done | bytes 1048592 | tf_op jit(solution)/shard_map/psum | solution.py:71
  52.4 1.3 convert_select_fusion
  60.5 2.8 broadcast_select_fusion.1
  63.6 5.2 fusion.24
  68.8 124.2 %all-reduce.15.cloned.1.call-done = f32[512,256]{1,0:T(8,128)} async-done(((f32[512,256]{1,0:T(8,128)}), f32[512,256]{1,0:T(8,128)}) %all-reduce.15.cloned.1.call-update) | async-done | bytes 524304 | tf_op jit(solution)/shard_map/psum | solution.py:85
  193.0 2.8 fusion.25
  195.9 131.1 %all-reduce.17.cloned.1.call-done = f32[512,256]{1,0:T(8,128)} async-done(((f32[512,256]{1,0:T(8,128)}), f32[512,256]{1,0:T(8,128)}) %all-reduce.17.cloned.1.call-update) | async-done | bytes 524304 | tf_op jit(solution)/shard_map/psum | solution.py:85
  327.0 1.1 select_select_fusion
  328.1 1.8 fusion.26
  330.0 130.8 %all-reduce.19.cloned.1.call-done = f32[512,256]{1,0:T(8,128)} async-done(((f32[512,256]{1,0:T(8,128)}), f32[512,256]{1,0:T(8,128)}) %all-reduce.19.cloned.1.call-update) | async-done | bytes 524304 | tf_op jit(solution)/shard_map/psum | solution.py:85
  460.8 1.8 fusion.27
  462.7 131.9 %all-reduce.21.cloned.1.call-done = f32[512,256]{1,0:T(8,128)} async-done(((f32[512,256]{1,0:T(8,128)}), f32[512,256]{1,0:T(8,128)}) %all-reduce.21.cloned.1.call-update) | async-done | bytes 524304 | tf_op jit(solution)/shard_map/psum | solution.py:85
  594.6 1.1 broadcast_select_fusion.6
  595.8 1.8 fusion.28
  597.7 130.8 %all-reduce.23.cloned.1.call-done = f32[512,256]{1,0:T(8,128)} async-done(((f32[512,256]{1,0:T(8,128)}), f32[512,256]{1,0:T(8,128)}) %all-reduce.23.cloned.1.call-update) | async-done | bytes 524304 | tf_op jit(solution)/shard_map/psum | solution.py:85
  729.5 2.6 fusion.29
  732.2 130.2 %all-reduce.25.cloned.1.call-done = f32[512,256]{1,0:T(8,128)} async-done(((f32[512,256]{1,0:T(8,128)}), f32[512,256]{1,0:T(8,128)}) %all-reduce.25.cloned.1.call-update) | async-done | bytes 524304 | tf_op jit(solution)/shard_map/psum | solution.py:85
  864.4 2.6 fusion.30
  867.0 11.2 all-reduce.29.cloned.1.call-start
  878.2 44.1 %fusion.95 = (f32[1,4096,1,1024]{3,2,1,0:T(1,128)}, f32[1,4096,1,1024]{3,2,1,0:T(1,128)}, f32[1,4096,1,1024]{3,2,1,0:T(1,128)}, f32[1,4096,1,1024]{3,2,1,0:T(1,128)}) fusion(f32[1,16384,1,1024]{3,2,1,0:T(1,128)} %param.2), kind=kLoop, calls=%fused_computation.173 | loop fusion | bytes 134217728 | tf_op jit(solution)/shard_map/slice | solution.py:110
  922.2 74.2 %all-reduce.27.cloned.1.call-done = f32[512,256]{1,0:T(8,128)} async-done(((f32[512,256]{1,0:T(8,128)}), f32[512,256]{1,0:T(8,128)}) %all-reduce.27.cloned.1.call-update) | async-done | bytes 524304 | tf_op jit(solution)/shard_map/psum | solution.py:85
  998.3 2.6 fusion.31
  1001.0 8.4 constant_dynamic-slice_fusion.3
  1009.4 3.2 copy.8
  1012.5 3.2 copy.9
  1015.7 3.2 copy.10
  1018.9 1.6 copy.11
  1020.4 110.0 %all-reduce.29.cloned.1.call-done = f32[512,256]{1,0:T(8,128)} async-done(((f32[512,256]{1,0:T(8,128)}), f32[512,256]{1,0:T(8,128)}) %all-reduce.29.cloned.1.call-update) | async-done | bytes 524304 | tf_op jit(solution)/shard_map/psum | solution.py:85
  1131.6 19.6 %fusion.12 = f32[4096,256]{0,1:T(8,128)S(1)} fusion(f32[1024,256]{1,0:T(8,128)S(1)} %pad_maximum_fusion.7, f32[1,4096,1,1024]{3,2,1,0:T(1,128)} %get-tuple-element.2), kind=kOutput, calls=%fused_computation.12 | convolution fusion | flops 6442450944 | bytes 22020096 | tf_op jit(solution)/shard_map/dot_general | solution.py:13
  1151.2 1.6 slice.264
  1153.9 14.2 %fusion.15 = f32[4096,256]{0,1:T(8,128)S(1)} fusion(f32[1024,256]{1,0:T(8,128)S(1)} %pad_maximum_fusion.7, f32[1,4096,1,1024]{3,2,1,0:T(1,128)S(1)} %bitcast.106), kind=kOutput, calls=%fused_computation.13 | convolution fusion | flops 6442450944 | bytes 22020096 | tf_op jit(solution)/shard_map/dot_general | solution.py:13
  1168.1 1.5 slice.272
  1169.6 1.6 copy-done.2
  1171.7 19.4 %fusion.18 = f32[4096,256]{0,1:T(8,128)S(1)} fusion(f32[1024,256]{1,0:T(8,128)S(1)} %pad_maximum_fusion.7, f32[1,4096,1,1024]{3,2,1,0:T(1,128)} %get-tuple-element.5), kind=kOutput, calls=%fused_computation.14 | convolution fusion | flops 6442450944 | bytes 22020096 | tf_op jit(solution)/shard_map/dot_general | solution.py:13
  1191.1 1.6 slice.280
  1194.0 14.3 %fusion.21 = f32[4096,256]{0,1:T(8,128)S(1)} fusion(f32[1024,256]{1,0:T(8,128)S(1)} %pad_maximum_fusion.7, f32[1,4096,1,1024]{3,2,1,0:T(1,128)S(1)} %bitcast.104), kind=kOutput, calls=%fused_computation.15 | convolution fusion | flops 6442450944 | bytes 22020096 | tf_op jit(solution)/shard_map/dot_general | solution.py:13
  1210.8 1.8 slice_add_fusion.3
  1213.0 1.5 collective-permute-start.1
  1214.8 1.9 slice_add_fusion.2
  1217.0 1.5 collective-permute-start.3
  1219.5 1.5 collective-permute-start.5
  1222.2 16.8 %collective-permute-done.1 = f32[2048,128]{0,1:T(8,128)S(1)} collective-permute-done((f32[2048,128]{0,1:T(8,128)S(1)}, f32[2048,128]{0,1:T(8,128)S(1)}, u32[]{:S(2)}, u32[]{:S(2)}) %collective-permute-start.1) | collective-permute-done | bytes 1048608 | tf_op jit(solution)/shard_map/ppermute | solution.py:114
  1239.3 22.3 %collective-permute-done.3 = f32[2048,128]{0,1:T(8,128)S(1)} collective-permute-done((f32[2048,128]{0,1:T(8,128)S(1)}, f32[2048,128]{0,1:T(8,128)S(1)}, u32[]{:S(2)}, u32[]{:S(2)}) %collective-permute-start.3) | collective-permute-done | bytes 1048608 | tf_op jit(solution)/shard_map/ppermute | solution.py:114
  1261.7 22.3 %collective-permute-done.5 = f32[2048,128]{0,1:T(8,128)S(1)} collective-permute-done((f32[2048,128]{0,1:T(8,128)S(1)}, f32[2048,128]{0,1:T(8,128)S(1)}, u32[]{:S(2)}, u32[]{:S(2)}) %collective-permute-start.5) | collective-permute-done | bytes 1048608 | tf_op jit(solution)/shard_map/ppermute | solution.py:114
  1284.2 21.6 %collective-permute-done.7 = f32[2048,128]{0,1:T(8,128)S(1)} collective-permute-done((f32[2048,128]{0,1:T(8,128)S(1)}, f32[2048,128]{0,1:T(8,128)S(1)}, u32[]{:S(2)}, u32[]{:S(2)}) %collective-permute-start.7) | collective-permute-done | bytes 1048608 | tf_op jit(solution)/shard_map/ppermute | solution.py:114
  1308.9 2.3 maximum_bitcast_fusion
  (131 shorter events, 27.1 us)
Async XLA Ops:
  7.2 45.2 %all-reduce.13.cloned.1.call-start = ((), (), s32[]{:S(2)}) async-start(), calls=%async_computation | async-start | bytes 2097152 | tf_op jit(solution)/shard_map/psum | solution.py:71
  10.3 1.3 copy-start.6
  13.2 179.8 %all-reduce.15.cloned.1.call-start = ((), (), s32[]{:S(2)}) async-start(), calls=%async_computation.1 | async-start | bytes 1048576 | tf_op jit(solution)/shard_map/psum | solution.py:85
  63.3 263.7 %all-reduce.17.cloned.1.call-start = ((), (), s32[]{:S(2)}) async-start(), calls=%async_computation.2 | async-start | bytes 1048576 | tf_op jit(solution)/shard_map/psum | solution.py:85
  195.9 264.9 %all-reduce.19.cloned.1.call-start = ((), (), s32[]{:S(2)}) async-start(), calls=%async_computation.3 | async-start | bytes 1048576 | tf_op jit(solution)/shard_map/psum | solution.py:85
  328.1 134.5 %copy-start.7 = (f32[512,256]{1,0:T(8,128)}, f32[512,256]{1,0:T(8,128)S(1)}, u32[]{:S(2)}) copy-start(f32[512,256]{1,0:T(8,128)S(1)} %select_select_fusion) | copy-start | bytes 1572868
  329.9 264.7 %all-reduce.21.cloned.1.call-start = ((), (), s32[]{:S(2)}) async-start(), calls=%async_computation.4 | async-start | bytes 1048576 | tf_op jit(solution)/shard_map/psum | solution.py:85
  462.6 265.8 %all-reduce.23.cloned.1.call-start = ((), (), s32[]{:S(2)}) async-start(), calls=%async_computation.5 | async-start | bytes 1048576 | tf_op jit(solution)/shard_map/psum | solution.py:85
  597.6 264.8 %all-reduce.25.cloned.1.call-start = ((), (), s32[]{:S(2)}) async-start(), calls=%async_computation.6 | async-start | bytes 1048576 | tf_op jit(solution)/shard_map/psum | solution.py:85
  732.2 264.2 %all-reduce.27.cloned.1.call-start = ((), (), s32[]{:S(2)}) async-start(), calls=%async_computation.7 | async-start | bytes 1048576 | tf_op jit(solution)/shard_map/psum | solution.py:85
  863.6 0.8 copy-start.10
  867.0 263.4 %all-reduce.29.cloned.1.call-start = ((), (), s32[]{:S(2)}) async-start(), calls=%async_computation.8 | async-start | bytes 1048576 | tf_op jit(solution)/shard_map/psum | solution.py:85
  997.5 0.8 copy-start.8
  1018.9 111.5 %copy-start.9 = (f32[512,256]{1,0:T(8,128)S(1)}, f32[512,256]{1,0:T(8,128)}, u32[]{:S(2)}) copy-start(f32[512,256]{1,0:T(8,128)} %copy-done.8) | copy-start | bytes 1572868
  1130.5 23.4 %slice-start.4 = ((s8[16777216]{0:T(1024)(128)(4,1)}), s8[4194304]{0:T(1024)(128)(4,1)S(1)}, s32[]{:S(2)}) async-start(s8[16777216]{0:T(1024)(128)(4,1)} %bitcast.105), calls=%async_computation.13 | async-start | bytes 8388608
  1131.6 22.3 %slice-start.5 = ((s8[16777216]{0:T(1024)(128)(4,1)}), s8[4194304]{0:T(1024)(128)(4,1)S(1)}, s32[]{:S(2)}) async-start(s8[16777216]{0:T(1024)(128)(4,1)} %bitcast.105), calls=%async_computation.14 | async-start | bytes 8388608
  1131.6 22.3 %slice-start.6 = ((s8[16777216]{0:T(1024)(128)(4,1)}), s8[4194304]{0:T(1024)(128)(4,1)S(1)}, s32[]{:S(2)}) async-start(s8[16777216]{0:T(1024)(128)(4,1)} %bitcast.105), calls=%async_computation.15 | async-start | bytes 8388608
  1131.6 22.3 %slice-start.7 = ((s8[16777216]{0:T(1024)(128)(4,1)}), s8[4194304]{0:T(1024)(128)(4,1)S(1)}, s32[]{:S(2)}) async-start(s8[16777216]{0:T(1024)(128)(4,1)} %bitcast.105), calls=%async_computation.16 | async-start | bytes 8388608
  1151.2 2.7 copy-start.4
  1153.9 56.0 %collective-permute-start = (f32[4096,128]{0,1:T(8,128)}, f32[4096,128]{0,1:T(8,128)}, u32[]{:S(2)}, u32[]{:S(2)}) collective-permute-start(f32[4096,128]{0,1:T(8,128)} %slice.264), channel_id=1, source_target_pairs={{0,1},{1,0},{2,3},{3,2},{4,5},{5,4},{6,7},{7,6},{8,9},{9,8},{10,11... | collective-permute-start | bytes 6291464 | tf_op jit(solution)/shard_map/ppermute | solution.py:111
  1168.1 3.1 copy-start.2
  1168.1 25.8 %slice-start = ((s8[16777216]{0:T(1024)(128)(4,1)}), s8[4194304]{0:T(1024)(128)(4,1)S(1)}, s32[]{:S(2)}) async-start(s8[16777216]{0:T(1024)(128)(4,1)} %bitcast.103), calls=%async_computation.9 | async-start | bytes 8388608
  1171.2 43.3 %collective-permute-start.2 = (f32[4096,128]{0,1:T(8,128)}, f32[4096,128]{0,1:T(8,128)}, u32[]{:S(2)}, u32[]{:S(2)}) collective-permute-start(f32[4096,128]{0,1:T(8,128)} %slice.272), channel_id=1, source_target_pairs={{0,1},{1,0},{2,3},{3,2},{4,5},{5,4},{6,7},{7,6},{8,9},{9,8},{10,11... | collective-permute-start | bytes 6291464 | tf_op jit(solution)/shard_map/ppermute | solution.py:111
  1171.7 22.2 %slice-start.1 = ((s8[16777216]{0:T(1024)(128)(4,1)}), s8[4194304]{0:T(1024)(128)(4,1)S(1)}, s32[]{:S(2)}) async-start(s8[16777216]{0:T(1024)(128)(4,1)} %bitcast.103), calls=%async_computation.10 | async-start | bytes 8388608
  1171.7 22.2 %slice-start.2 = ((s8[16777216]{0:T(1024)(128)(4,1)}), s8[4194304]{0:T(1024)(128)(4,1)S(1)}, s32[]{:S(2)}) async-start(s8[16777216]{0:T(1024)(128)(4,1)} %bitcast.103), calls=%async_computation.11 | async-start | bytes 8388608
  1171.7 22.2 %slice-start.3 = ((s8[16777216]{0:T(1024)(128)(4,1)}), s8[4194304]{0:T(1024)(128)(4,1)S(1)}, s32[]{:S(2)}) async-start(s8[16777216]{0:T(1024)(128)(4,1)} %bitcast.103), calls=%async_computation.12 | async-start | bytes 8388608
  1191.1 2.6 copy-start
  1193.7 24.8 %collective-permute-start.4 = (f32[4096,128]{0,1:T(8,128)}, f32[4096,128]{0,1:T(8,128)S(1)}, u32[]{:S(2)}, u32[]{:S(2)}) collective-permute-start(f32[4096,128]{0,1:T(8,128)} %slice.280), channel_id=1, source_target_pairs={{0,1},{1,0},{2,3},{3,2},{4,5},{5,4},{6,7},{7,6},{8,9},{9,8},{10,11... | collective-permute-start | bytes 6291464 | tf_op jit(solution)/shard_map/ppermute | solution.py:111
  1208.2 2.6 copy-start.5
  1208.4 12.6 collective-permute-start.6
  1212.6 2.2 copy-start.3
  1213.0 26.1 %collective-permute-start.1 = (f32[2048,128]{0,1:T(8,128)S(1)}, f32[2048,128]{0,1:T(8,128)S(1)}, u32[]{:S(2)}, u32[]{:S(2)}) collective-permute-start(f32[2048,128]{0,1:T(8,128)S(1)} %pad_maximum_fusion.8), channel_id=1, source_target_pairs={{0,2},{1,3},{2,0},{3,1},{4,6},{5,7},{6,4},{7,5},{8,10},{9,11},{10,... | collective-permute-start | bytes 3145736 | tf_op jit(solution)/shard_map/ppermute | solution.py:114
  1216.7 2.2 copy-start.1
  1217.0 44.5 %collective-permute-start.3 = (f32[2048,128]{0,1:T(8,128)S(1)}, f32[2048,128]{0,1:T(8,128)S(1)}, u32[]{:S(2)}, u32[]{:S(2)}) collective-permute-start(f32[2048,128]{0,1:T(8,128)S(1)} %pad_maximum_fusion.9), channel_id=1, source_target_pairs={{0,2},{1,3},{2,0},{3,1},{4,6},{5,7},{6,4},{7,5},{8,10},{9,11},{10,... | collective-permute-start | bytes 3145736 | tf_op jit(solution)/shard_map/ppermute | solution.py:114
  1219.5 64.5 %collective-permute-start.5 = (f32[2048,128]{0,1:T(8,128)S(1)}, f32[2048,128]{0,1:T(8,128)S(1)}, u32[]{:S(2)}, u32[]{:S(2)}) collective-permute-start(f32[2048,128]{0,1:T(8,128)S(1)} %pad_maximum_fusion.10), channel_id=1, source_target_pairs={{0,2},{1,3},{2,0},{3,1},{4,6},{5,7},{6,4},{7,5},{8,10},{9,11},{10,... | collective-permute-start | bytes 3145736 | tf_op jit(solution)/shard_map/ppermute | solution.py:114
  1221.6 84.2 %collective-permute-start.7 = (f32[2048,128]{0,1:T(8,128)S(1)}, f32[2048,128]{0,1:T(8,128)S(1)}, u32[]{:S(2)}, u32[]{:S(2)}) collective-permute-start(f32[2048,128]{0,1:T(8,128)S(1)} %pad_maximum_fusion.11), channel_id=1, source_target_pairs={{0,2},{1,3},{2,0},{3,1},{4,6},{5,7},{6,4},{7,5},{8,10},{9,11},{10,... | collective-permute-start | bytes 3145736 | tf_op jit(solution)/shard_map/ppermute | solution.py:114
  1305.8 1.2 copy-start.14
  1306.1 1.3 copy-start.13
  1307.1 1.3 copy-start.12
  1307.5 1.3 copy-start.11
Sparse Core Ops, SparseCore 0:
  13.3 38.9 all-reduce.12
  63.4 129.5 all-reduce.14
  198.9 128.0 all-reduce.16
  332.7 128.0 all-reduce.18
  466.5 128.0 all-reduce.20
  600.3 128.0 all-reduce.22
  734.3 128.0 all-reduce.24
  868.3 128.0 all-reduce.26
  1002.3 128.0 all-reduce.28
